TPU v7x, 128 devices: a whole 4x4x4 slice. The times are simulated.
128 devices in a mesh: seq: 32 (over x, z, core), head: 4 (over y).
Axes of the slice: x: 4, y: 4, z: 4, core: 2. Of those that a mesh axis runs over, the one named last changes fastest.
Arguments:
- q_in: bfloat16 [65536, 2048], P(('seq', 'head')), may hold values from -6 to 6
- k_in: bfloat16 [65536, 2048], P(('seq', 'head')), may hold values from -6 to 6
- v_in: bfloat16 [65536, 2048], P(('seq', 'head')), may hold values from -6 to 6
- beta: bfloat16 [65536, 16], P(('seq', 'head')), may hold values from 0 to 1, as said below
- conv_q: float32 [4, 2048], replicated, may hold values from -3 to 3
- conv_k: float32 [4, 2048], replicated, may hold values from -3 to 3
- conv_v: float32 [4, 2048], replicated, may hold values from -3 to 3
- out_gain: float32 [128], replicated, may hold values from 0.25 to 1.75
Outputs:
- mixed: bfloat16 [65536, 2048], P(('seq', 'head'))
Inputs may be any that keep to these rules, and one draw needn't show every extreme that they name: `beta`: write strengths of the delta rule, positive.
All inputs are finite; a program needn't handle non-finite values.
Results may differ from a plain program's by a relative error of at most 0.001.
Values may be sent and summed in bfloat16 or wider, within the bound.
No kernel may reach another device: no remote copies, remote signals or barrier semaphores. Data moves between devices by JAX's collectives and lax.ppermute only.
A program may use at most 576 MiB of HBM per device.

v0:
```python
import jax
import jax.numpy as jnp
from jax import lax
from jax.sharding import PartitionSpec as P

KEY_WIDTH = 128
DV = 128
BLOCK = 64
KW = 4


peak_level = lax.Precision.HIGHEST


def shifted(value, axis, by):
    peers = lax.axis_size(axis)
    pairs = [(i, i + by) for i in range(peers) if 0 <= i + by < peers]
    return lax.ppermute(value, axis, pairs)


def causal_conv(padded, weight, length):
    summed = weight[0] * padded[0:length]
    for offset in range(1, weight.shape[0]):
        summed = summed + weight[offset] * padded[offset : offset + length]
    return summed


def unit_rows(vectors):
    return vectors / jnp.sqrt(jnp.sum(vectors * vectors, axis=-1, keepdims=True) + 1e-06)


def features(q_pad, k_pad, v_pad, beta_rows, conv_q, conv_k, conv_v):
    length = beta_rows.shape[0]
    head_count = beta_rows.shape[1]
    q_conv = causal_conv(q_pad.astype(jnp.float32), conv_q, length)
    k_conv = causal_conv(k_pad.astype(jnp.float32), conv_k, length)
    v_conv = causal_conv(v_pad.astype(jnp.float32), conv_v, length)
    queries = unit_rows(jax.nn.silu(q_conv).reshape(length, head_count, -1))
    key_rows = unit_rows(jax.nn.silu(k_conv).reshape(length, head_count, -1))
    values = jax.nn.silu(v_conv).reshape(length, head_count, -1)
    return (queries, key_rows, values, beta_rows.astype(jnp.float32))


def block_parts(queries, key_rows, values, surge_strength):
    length, head_count, ignored = key_rows.shape
    block_count = length // BLOCK

    def to_blocks(matrix):
        return jnp.swapaxes(matrix.reshape(block_count, BLOCK, head_count, matrix.shape[-1]), 1, 2)

    query_tiles = to_blocks(queries)
    key_tiles = to_blocks(key_rows)
    v_blocks = to_blocks(values)
    s_blocks = jnp.swapaxes(surge_strength.reshape(block_count, BLOCK, head_count), 1, 2)[..., None]
    scaled_k = key_tiles * s_blocks
    gram_rows = jnp.einsum("nhik,nhjk->nhij", scaled_k, key_tiles, precision=peak_level)
    system = jnp.tril(gram_rows, -1) + jnp.eye(BLOCK, dtype=gram_rows.dtype)
    weight_rows = lax.linalg.triangular_solve(
        system, scaled_k, left_side=True, lower=True, unit_diagonal=True
    )
    update_rows = lax.linalg.triangular_solve(
        system, v_blocks * s_blocks, left_side=True, lower=True, unit_diagonal=True
    )
    attention_scores = jnp.tril(
        jnp.einsum("nhik,nhjk->nhij", query_tiles, key_tiles, precision=peak_level)
    )
    return (query_tiles, key_tiles, weight_rows, update_rows, attention_scores)


def run_blocks(carried, parts):

    def run_advance(present_value, pieces):
        query_tiles, key_tiles, weight_rows, update_rows, attention_scores = pieces
        fresh_values = update_rows - jnp.einsum(
            "jel,jlm->jem", weight_rows, present_value, precision=peak_level
        )
        blended_rows = jnp.einsum(
            "jel,jlm->jem", query_tiles, present_value, precision=peak_level
        ) + jnp.einsum("ezq,eqd->ezd", attention_scores, fresh_values, precision=peak_level)
        present_value = present_value + jnp.einsum(
            "pty,ptn->pyn", key_tiles, fresh_values, precision=peak_level
        )
        return (present_value, blended_rows)

    ignored, outputs = lax.scan(run_advance, carried, parts)
    block_count, head_count, rows_block, width = outputs.shape
    return jnp.swapaxes(outputs, 1, 2).reshape(block_count * rows_block, head_count, width)


def finish(outputs, out_gain):
    inv_rms = lax.rsqrt(jnp.mean(outputs * outputs, axis=-1, keepdims=True) + 1e-05)
    return (outputs * inv_rms * out_gain).reshape(outputs.shape[0], -1).astype(jnp.bfloat16)


def identity_pair(head_count):
    eye_block = jnp.broadcast_to(
        jnp.eye(KEY_WIDTH, dtype=jnp.float32), (head_count, KEY_WIDTH, KEY_WIDTH)
    )
    return (eye_block, jnp.zeros((head_count, KEY_WIDTH, DV), jnp.float32))


def summarize(parts, head_count):

    def summarize_advance(carried, pieces):
        transfer, shifted_state = carried
        query_tiles, key_tiles, weight_rows, update_rows, attention_scores = pieces
        fresh_values = update_rows - jnp.einsum(
            "jel,jlm->jem", weight_rows, shifted_state, precision=peak_level
        )
        shifted_state = shifted_state + jnp.einsum(
            "pty,ptn->pyn", key_tiles, fresh_values, precision=peak_level
        )
        moved = jnp.einsum("hck,hkj->hcj", weight_rows, transfer, precision=peak_level)
        transfer = transfer - jnp.einsum("hck,hcj->hkj", key_tiles, moved, precision=peak_level)
        return ((transfer, shifted_state), None)

    summary, ignored = lax.scan(summarize_advance, identity_pair(head_count), parts)
    return summary


def local_parts(q_rows, k_rows, v_rows, beta_rows, rims, conv_q, conv_k, conv_v):
    q_pad = jnp.concatenate([rims[0], q_rows], axis=0)
    k_pad = jnp.concatenate([rims[1], k_rows], axis=0)
    v_pad = jnp.concatenate([rims[2], v_rows], axis=0)
    return block_parts(*features(q_pad, k_pad, v_pad, beta_rows, conv_q, conv_k, conv_v))


def shards(q_in, k_in, v_in, beta, conv_q, conv_k, conv_v, out_gain):
    edge = KW - 1
    q_rows, k_rows, v_rows, beta_rows = (
        lax.all_to_all(q_in, "head", split_axis=1, concat_axis=0, tiled=True),
        lax.all_to_all(k_in, "head", split_axis=1, concat_axis=0, tiled=True),
        lax.all_to_all(v_in, "head", split_axis=1, concat_axis=0, tiled=True),
        lax.all_to_all(beta, "head", split_axis=1, concat_axis=0, tiled=True),
    )
    local_heads = beta_rows.shape[1]
    start = lax.axis_index("head") * (local_heads * KEY_WIDTH)
    conv_qh = lax.dynamic_slice_in_dim(conv_q, start, local_heads * KEY_WIDTH, 1)
    conv_kh = lax.dynamic_slice_in_dim(conv_k, start, local_heads * KEY_WIDTH, 1)
    conv_vh = lax.dynamic_slice_in_dim(conv_v, start, local_heads * DV, 1)
    rim_stack = jnp.stack([q_rows[-edge:], k_rows[-edge:], v_rows[-edge:]])
    rims = shifted(rim_stack, "seq", 1)
    parts = local_parts(q_rows, k_rows, v_rows, beta_rows, rims, conv_qh, conv_kh, conv_vh)
    transfer, shifted_state = summarize(parts, local_heads)

    def forward(turn, incoming):
        outgoing = (
            jnp.einsum("hij,hjv->hiv", transfer, incoming, precision=peak_level) + shifted_state
        )
        return shifted(outgoing, "seq", 1)

    incoming = lax.fori_loop(0, lax.axis_size("seq") - 1, forward, jnp.zeros_like(shifted_state))
    normed = finish(run_blocks(incoming, parts), out_gain)
    return lax.all_to_all(normed, "head", split_axis=0, concat_axis=1, tiled=True)


def solution(mesh):
    in_specs = (
        P(("seq", "head"), None),
        P(("seq", "head"), None),
        P(("seq", "head"), None),
        P(("seq", "head"), None),
        P(),
        P(),
        P(),
        P(),
    )
    out_specs = P(("seq", "head"), None)
    return jax.shard_map(shards, mesh=mesh, in_specs=in_specs, out_specs=out_specs, check_vma=False)
```

profile of v0, /device:TPU:2, one launch (start us, length us, event | category | flops | bytes accessed | tf_op | source)
XLA Modules:
  0.0 1281.7 jit_solution(11042192531841803919)
XLA Ops:
  12.3 22.4 %all-to-all-done.1 = bf16[512,4,512]{0,2,1:T(8,128)(2,1)S(1)} async-done(((bf16[512,4,512]{0,2,1:T(8,128)(2,1)}), bf16[512,4,512]{0,2,1:T(8,128)(2,1)S(1)}, u32[]{:S(2)}, u32[]{:S(2)}) %all-to-all-start.1) | async-done | bytes 2097184 | tf_op jit(solution)/shard_map/all_to_all | solution.py:132
  43.1 21.5 %all-to-all-done.2 = bf16[512,4,512]{0,2,1:T(8,128)(2,1)} async-done(((bf16[512,4,512]{0,2,1:T(8,128)(2,1)}), bf16[512,4,512]{0,2,1:T(8,128)(2,1)}, u32[]{:S(2)}, u32[]{:S(2)}) %all-to-all-start.2) | async-done | bytes 2097184 | tf_op jit(solution)/shard_map/all_to_all | solution.py:133
  80.0 13.7 %all-to-all-done = bf16[512,4,512]{0,2,1:T(8,128)(2,1)} async-done(((bf16[512,4,512]{0,2,1:T(8,128)(2,1)}), bf16[512,4,512]{0,2,1:T(8,128)(2,1)}, u32[]{:S(2)}, u32[]{:S(2)}) %all-to-all-start) | async-done | bytes 2097184 | tf_op jit(solution)/shard_map/all_to_all | solution.py:131
  173.4 8.4 fusion.56
  202.7 12.4 fusion.34
  222.5 7.9 add_bitcast_fusion
  230.4 265.2 %custom-call.5 = f32[32,4,1,64,64]{0,3,4,2,1:T(8,128)} custom-call(f32[32,4,1,64,64]{0,4,3,2,1:T(8,128)} %add_bitcast_fusion), custom_call_target="InvertDiagBlocksLowerTriangular" | custom-call | tf_op jit(solution)/shard_map/triangular_solve/custom-call.1 | solution.py:58
  495.6 8.7 copy.138
  514.2 9.9 fusion.32
  530.2 182.0 %while.37 = (s32[]{:T(128)}, f32[4,128,128]{2,1,0:T(8,128)S(1)}, f32[4,128,128]{2,1,0:T(8,128)S(1)}, f32[32,4,64,128]{3,2,1,0:T(8,128)}, f32[32,4,64,128]{3,2,1,...) while((s32[]{:T(128)}, f32[4,128,128]{2,1,0:T(8,128)S(1)}, ...), condition=%wide.region_2.4_spmd.clone, body=%wide.region_1.0_spmd.clone.sunk | while | flops 201621504 | bytes 2755168 | solution.py:117
  712.2 316.4 %while.35 = (s32[]{:T(128)}, f32[4,128,128]{2,1,0:T(8,128)S(1)}, f32[4,128,128]{2,1,0:T(8,128)S(1)}, f32[4,128,128]{2,1,0:T(8,128)S(1)}, s32[]{:T(128)}) while((s32[]{:T(128)}, f32[4,128,128]{2,1,0:T(8,128)S(1)}, f32[4,128,128]{2,1,0:T(8,128)S(1)}, f32[4,128,128]{2,1,0:T(8,128)S(1)}, s32[]{:T(128)}) %tuple.81), condition=%wide.region_4.6_spmd, body=%wide.region_3.5_spmd.sunk | while | flops 100728832 | bytes 2097253 | solution.py:152
  714.6 7.9 collective-permute-done
  724.8 7.9 collective-permute-done
  735.0 7.9 collective-permute-done
  745.2 7.9 collective-permute-done
  755.4 7.9 collective-permute-done
  765.6 7.9 collective-permute-done
  775.8 7.9 collective-permute-done
  786.0 7.9 collective-permute-done
  796.2 7.9 collective-permute-done
  806.4 7.9 collective-permute-done
  816.6 7.9 collective-permute-done
  826.8 7.9 collective-permute-done
  837.1 7.9 collective-permute-done
  847.3 7.9 collective-permute-done
  857.5 7.9 collective-permute-done
  867.7 7.9 collective-permute-done
  877.9 7.9 collective-permute-done
  888.1 7.9 collective-permute-done
  898.3 7.9 collective-permute-done
  1028.6 190.8 %while.36 = (s32[]{:T(128)}, f32[4,128,128]{2,1,0:T(8,128)S(1)}, f32[32,4,64,128]{3,2,1,0:T(8,128)}, f32[32,4,64,128]{3,2,1,0:T(8,128)}, f32[32,4,64,128]{3,2,1,...) while((s32[]{:T(128)}, f32[4,128,128]{2,1,0:T(8,128)S(1)}, ...), condition=%wide.region_7.9_spmd, body=%wide.region_6.8_spmd.sunk | while | flops 176291840 | bytes 2493533 | solution.py:85
  1250.5 24.7 %all_to_all.86 = bf16[4,512,512]{2,1,0:T(8,128)(2,1)S(1)} all-to-all(bf16[4,512,512]{2,1,0:T(8,128)(2,1)S(1)} %multiply_convert_fusion), channel_id=1, replica_groups=mesh['seq'=32,'head'=4] {'head'}, dimensions={0} | all-to-all | bytes 4194304 | tf_op jit(solution)/shard_map/all_to_all | solution.py:154
  (428 shorter events, 733.6 us)
Async XLA Ops:
  3.9 30.8 %all-to-all-start.1 = ((bf16[512,4,512]{0,2,1:T(8,128)(2,1)}), bf16[512,4,512]{0,2,1:T(8,128)(2,1)S(1)}, u32[]{:S(2)}, u32[]{:S(2)}) async-start(bf16[512,4,512]{0,2,1:T(8,128)(2,1)} %bitcast.158), calls=%async_computation.1 | async-start | bytes 4194304 | tf_op jit(solution)/shard_map/all_to_all | solution.py:132
  34.7 29.9 %all-to-all-start.2 = ((bf16[512,4,512]{0,2,1:T(8,128)(2,1)}), bf16[512,4,512]{0,2,1:T(8,128)(2,1)}, u32[]{:S(2)}, u32[]{:S(2)}) async-start(bf16[512,4,512]{0,2,1:T(8,128)(2,1)} %bitcast.157), calls=%async_computation.2 | async-start | bytes 4194304 | tf_op jit(solution)/shard_map/all_to_all | solution.py:133
  64.7 29.0 %all-to-all-start = ((bf16[512,4,512]{0,2,1:T(8,128)(2,1)}), bf16[512,4,512]{0,2,1:T(8,128)(2,1)}, u32[]{:S(2)}, u32[]{:S(2)}) async-start(bf16[512,4,512]{0,2,1:T(8,128)(2,1)} %bitcast.156), calls=%async_computation | async-start | bytes 4194304 | tf_op jit(solution)/shard_map/all_to_all | solution.py:131
  93.7 10.9 all-to-all-start.3
  712.6 9.8 collective-permute-start
  722.9 9.8 collective-permute-start
  733.1 9.8 collective-permute-start
  743.3 9.8 collective-permute-start
  753.5 9.8 collective-permute-start
  763.7 9.8 collective-permute-start
  773.9 9.8 collective-permute-start
  784.1 9.8 collective-permute-start
  794.3 9.8 collective-permute-start
  804.5 9.8 collective-permute-start
  814.7 9.8 collective-permute-start
  824.9 9.8 collective-permute-start
  835.1 9.8 collective-permute-start
  845.3 9.8 collective-permute-start
  855.5 9.8 collective-permute-start
  865.7 9.8 collective-permute-start
  875.9 9.8 collective-permute-start
  886.2 9.8 collective-permute-start
  896.4 9.8 collective-permute-start
  906.6 9.8 collective-permute-start
  916.8 9.8 collective-permute-start
  927.0 9.8 collective-permute-start
  937.2 9.8 collective-permute-start
  947.4 9.8 collective-permute-start
  957.6 9.8 collective-permute-start
  967.8 9.8 collective-permute-start
  978.0 9.8 collective-permute-start
  1018.8 9.8 collective-permute-start
  (19 other events, 207.9 us)
where the time goes:
time: 1290 us; the launch traced here: 1280 us
  matrix products  419 us (32%)
  other arithmetic  329 us (26%)
  waiting for transfers between devices  306 us (24%)
  local copies, waits for them, and re-layouts  120 us (9%)
  starting transfers between devices  78.2 us (6%)
  blocking collectives  24.7 us (2%)
    another operation x5, other arithmetic, block_parts(): lax.linalg.triangular_solve(system, scaled_k, left_side=True, lower=True,...  274 us
    ppermute x32, waiting for transfers between devices, shifted(): return lax.ppermute(value, axis, pairs)  249 us
    ppermute x32, starting transfers between devices, shifted(): return lax.ppermute(value, axis, pairs)  61.6 us
    dot_general x32, matrix products, run_advance(): jnp.einsum('jel,jlm->jem', query_tiles, present_value, precision=peak_level)  61.6 us
    dot_general x32, matrix products, summarize_advance(): jnp.einsum('pty,ptn->pyn', key_tiles, fresh_values, precision=peak_level)  48.9 us
    dot_general x32, matrix products, summarize_advance(): jnp.einsum('hck,hcj->hkj', key_tiles, moved, precision=peak_level)  48.6 us
    dot_general x32, matrix products, run_advance(): jnp.einsum('pty,ptn->pyn', key_tiles, fresh_values, precision=peak_level)  48.3 us
    dot_general x32, matrix products, run_advance(): jnp.einsum('jel,jlm->jem', weight_rows, present_value, precision=peak_level)  42.5 us
  transfers between devices with their start and end apart: 36, of which 35 were waited for; matrix products, arithmetic and copies ran while one was open for 2% of the time, Pallas kernels for 0%

commit v1 on v0

v1 whole, which is shorter than its diff:
```python
import functools

import jax
import jax.numpy as jnp
from jax import lax
from jax.experimental import pallas as pl
from jax.experimental.pallas import tpu as pltpu
from jax.sharding import Mesh, PartitionSpec as P

WIDTH = 128
BLOCK = 64
KW = 4
F32 = jnp.float32
BF16 = jnp.bfloat16
HEADS_PER_STEP = 4
HEADS_PER_END = 4


def dot(a, b, ca, cb):
    return lax.dot_general(a, b, (((ca,), (cb,)), ((), ())), preferred_element_type=F32)


def split(x):
    high = x.astype(BF16)
    return high, (x - high.astype(F32)).astype(BF16)


def cat(parts, axis):
    return jnp.concatenate(parts, axis=axis)


def mm_wide(a, b, cb):
    ah, al = a
    bh, bl = b
    return dot(cat([ah, al], 1), cat([bh, bh], cb), 1, cb) + dot(ah, bl, 1, cb)


def left(a):
    return cat([a[0], a[0], a[1]], 1)


def right(b):
    return cat([b[0], b[1], b[0]], 0)


def front_kernel(heads, q_ref, k_ref, v_ref, rim_ref, beta_ref, cq_ref, ck_ref, cv_ref, tb_ref, qe_ref, ol_ref, pad_ref):
    length = q_ref.shape[0]
    blocks = length // BLOCK
    edge = KW - 1

    def feature(slot, x_ref, w_ref):
        pad = pad_ref.at[slot]
        pad[8 - edge : 8, :] = rim_ref[slot * edge : (slot + 1) * edge, :].astype(F32)
        pad[8:, :] = x_ref[...].astype(F32)
        total = w_ref[0:1, :] * pad[8 - edge : 8 - edge + length, :]
        for j in range(1, KW):
            total = total + w_ref[j : j + 1, :] * pad[8 - edge + j : 8 - edge + j + length, :]
        return total / (1.0 + jnp.exp(-total))

    def unit(x):
        return x * lax.rsqrt(jnp.sum(x * x, axis=-1, keepdims=True) + 1e-06)

    q_all = feature(0, q_ref, cq_ref)
    k_all = feature(1, k_ref, ck_ref)
    v_all = feature(2, v_ref, cv_ref)
    beta = beta_ref[...].astype(F32)
    lane = lax.broadcasted_iota(jnp.int32, beta.shape, 1)
    row = lax.broadcasted_iota(jnp.int32, (BLOCK, BLOCK), 0)
    col = lax.broadcasted_iota(jnp.int32, (BLOCK, BLOCK), 1)
    one = jnp.where(row == col, 1.0, 0.0).astype(F32)
    masks = [
        ((row >> (n + 1)) == (col >> (n + 1))) & (((row >> n) & 1) == 1) & (((col >> n) & 1) == 0)
        for n in range(6)
    ]
    wide_row = lax.broadcasted_iota(jnp.int32, (WIDTH, 2 * WIDTH), 0)
    wide_col = lax.broadcasted_iota(jnp.int32, (WIDTH, 2 * WIDTH), 1)
    wide_one = jnp.where(wide_row == wide_col, 1.0, 0.0).astype(F32)

    units = [(i, c) for i in range(heads) for c in range(blocks)]
    q, k, kv_scaled, b = {}, {}, {}, {}
    for i in range(heads):
        lanes = slice(i * WIDTH, (i + 1) * WIDTH)
        qh, kh, vh = unit(q_all[:, lanes]), unit(k_all[:, lanes]), v_all[:, lanes]
        bh = jnp.sum(jnp.where(lane == pl.program_id(0) * heads + i, beta, 0.0), axis=1, keepdims=True)
        for c in range(blocks):
            rows = slice(c * BLOCK, (c + 1) * BLOCK)
            q[i, c], k[i, c], b[i, c] = qh[rows], kh[rows], bh[rows]
            kv_scaled[i, c] = cat([kh[rows] * bh[rows], vh[rows] * bh[rows]], 1)
    ks = {u: split(k[u]) for u in units}
    gram, score, inv = {}, {}, {}
    for u in units:
        both = mm_wide(split(cat([k[u], q[u]], 0)), ks[u], 1)
        gram[u] = both[:BLOCK] * b[u]
        score[u] = jnp.where(row >= col, both[BLOCK:], 0.0)
        inv[u] = one - jnp.where(masks[0], gram[u], 0.0)
    for n in range(1, 6):
        parts = {u: split(inv[u]) for u in units}
        moved = {u: dot(left(split(jnp.where(masks[n], gram[u], 0.0))), right(parts[u]), 1, 0) for u in units}
        inv = {u: inv[u] - dot(left(parts[u]), right(split(moved[u])), 1, 0) for u in units}
    step, extra, eff, local = {}, {}, {}, {}
    for u in units:
        solved = dot(left(split(inv[u])), right(split(kv_scaled[u])), 1, 0)
        signed = cat([-solved[:, :WIDTH], solved[:, WIDTH:]], 1)
        rhs = right(split(signed))
        kh, kl = ks[u]
        both = wide_one + dot(cat([kh, kh, kl], 0), rhs, 0, 0)
        step[u], extra[u] = both[:, :WIDTH], both
        seen = dot(left(split(score[u])), rhs, 1, 0)
        eff[u], local[u] = q[u] + seen[:, :WIDTH], seen[:, WIDTH:]
    state = {}
    for c in range(blocks):
        rows = slice(c * BLOCK, (c + 1) * BLOCK)
        for i in range(heads):
            lanes = slice(i * WIDTH, (i + 1) * WIDTH)
            u = (i, c)
            if c == 0:
                state[i] = extra[u]
                qe_ref[rows, lanes] = eff[u]
                ol_ref[rows, lanes] = local[u]
                continue
            out = mm_wide(split(cat([step[u], eff[u]], 0)), split(state[i]), 0)
            state[i] = cat([out[:WIDTH, :WIDTH], out[:WIDTH, WIDTH:] + extra[u][:, WIDTH:]], 1)
            qe_ref[rows, lanes] = out[WIDTH:, :WIDTH]
            ol_ref[rows, lanes] = out[WIDTH:, WIDTH:] + local[u]
    half = WIDTH // 2
    for i in range(heads):
        turned = state[i][:, :WIDTH].T
        added = state[i][:, WIDTH:].T
        for s in range(2):
            tb_ref[2 * i + s, :WIDTH, :] = turned
            tb_ref[2 * i + s, WIDTH:, :] = added[s * half : (s + 1) * half]


def joined(first, second):
    out = mm_wide(split(first), split(second[:WIDTH]), 0)
    return out[:WIDTH], out[WIDTH:] + second[WIDTH:]


def gather_kernel(group, seg_ref, loc_ref, grp_ref):
    groups = seg_ref.shape[0] // group
    for g in range(groups):
        loc_ref[g * group] = seg_ref[g * group]
    for j in range(1, group):
        for g in range(groups):
            at = g * group + j
            top, low = joined(loc_ref[at - 1], seg_ref[at])
            loc_ref[at, :WIDTH, :] = top
            loc_ref[at, WIDTH:, :] = low
    run = loc_ref[group - 1]
    grp_ref[0] = run
    for g in range(1, groups):
        run = cat(joined(run, loc_ref[g * group + group - 1]), 0)
        grp_ref[g] = run


def spread_kernel(group, loc_ref, grp_ref, far_ref, out_ref):
    groups = loc_ref.shape[0] // group
    reach = far_ref.shape[0]

    def through(state, place):
        return mm_wide(split(state), split(place[:WIDTH]), 0) + place[WIDTH:]

    begin = far_ref[reach - 1, WIDTH:, :]
    for d in range(reach - 2, -1, -1):
        begin = through(begin, far_ref[d])
    heads_of = [begin] + [through(begin, grp_ref[g]) for g in range(groups - 1)]
    for g in range(groups):
        out_ref[g * group] = heads_of[g]
    for g in range(groups):
        for j in range(1, group):
            out_ref[g * group + j] = through(heads_of[g], loc_ref[g * group + j - 1])


def end_kernel(heads, qe_ref, ol_ref, st_ref, gain_ref, out_ref):
    for i in range(heads):
        lanes = slice(i * WIDTH, (i + 1) * WIDTH)
        full = ol_ref[:, lanes] + mm_wide(split(qe_ref[:, lanes]), split(st_ref[i]), 1)
        mean = jnp.mean(full * full, axis=-1, keepdims=True)
        out_ref[:, lanes] = (full * lax.rsqrt(mean + 1e-05) * gain_ref[...]).astype(BF16)


def shards(sizes, q_in, k_in, v_in, beta, conv_q, conv_k, conv_v, out_gain):
    nx, nz, nc, ny = sizes
    edge = KW - 1
    length, width = q_in.shape
    head_count = beta.shape[1]
    pieces = 2 * head_count
    every = nx * nz * nc * ny
    rim = cat([q_in[-edge:], k_in[-edge:], v_in[-edge:]], 0)
    rim = lax.ppermute(rim, ("x", "z", "c", "y"), [(i, i + 1) for i in range(every - 1)])

    heads = min(HEADS_PER_STEP, head_count)
    wide = heads * WIDTH
    body = pl.BlockSpec((length, wide), lambda i: (0, i))
    taps = pl.BlockSpec((KW, wide), lambda i: (0, i))
    rows = WIDTH + WIDTH // 2
    vmem = pltpu.CompilerParams(vmem_limit_bytes=56 << 20)
    segment, qe, ol = pl.pallas_call(
        functools.partial(front_kernel, heads),
        grid=(head_count // heads,),
        in_specs=[body, body, body, pl.BlockSpec((3 * edge, wide), lambda i: (0, i)),
                  pl.BlockSpec((length, head_count), lambda i: (0, 0)), taps, taps, taps],
        out_specs=[pl.BlockSpec((2 * heads, rows, WIDTH), lambda i: (i, 0, 0)), body, body],
        out_shape=[jax.ShapeDtypeStruct((pieces, rows, WIDTH), F32),
                   jax.ShapeDtypeStruct((length, width), F32),
                   jax.ShapeDtypeStruct((length, width), F32)],
        scratch_shapes=[pltpu.VMEM((3, 8 + length, wide), F32)],
        compiler_params=vmem,
    )(q_in, k_in, v_in, rim, beta, conv_q, conv_k, conv_v)

    around = ("z", "c", "y")
    segment = lax.all_to_all(segment, around, 0, 0, tiled=True)
    loc, grp = pl.pallas_call(
        functools.partial(gather_kernel, ny),
        out_shape=[jax.ShapeDtypeStruct((pieces, rows, WIDTH), F32),
                   jax.ShapeDtypeStruct((pieces // ny, rows, WIDTH), F32)],
        compiler_params=vmem,
    )(segment)
    total = grp[-1]
    far = jnp.stack([
        lax.ppermute(total, "x", [(i, i + d) for i in range(nx - d)]) for d in range(1, nx)
    ])
    states = pl.pallas_call(
        functools.partial(spread_kernel, ny),
        out_shape=jax.ShapeDtypeStruct((pieces, WIDTH // 2, WIDTH), F32),
        compiler_params=vmem,
    )(loc, grp, far)
    states = lax.all_to_all(states, around, 0, 0, tiled=True).reshape(head_count, WIDTH, WIDTH)

    heads = min(HEADS_PER_END, head_count)
    body = pl.BlockSpec((length, heads * WIDTH), lambda i: (0, i))
    return pl.pallas_call(
        functools.partial(end_kernel, heads),
        grid=(head_count // heads,),
        in_specs=[body, body, pl.BlockSpec((heads, WIDTH, WIDTH), lambda i: (i, 0, 0)),
                  pl.BlockSpec((1, WIDTH), lambda i: (0, 0))],
        out_specs=body,
        out_shape=jax.ShapeDtypeStruct((length, width), BF16),
        compiler_params=vmem,
    )(qe, ol, states, out_gain.reshape(1, WIDTH))


def solution(mesh):
    sizes = (4, 4, 2, 4)
    axes = ("x", "z", "c", "y")
    fine = Mesh(mesh.devices.reshape(sizes), axes)
    rows = P(axes, None)
    return jax.shard_map(
        functools.partial(shards, sizes), mesh=fine,
        in_specs=(rows, rows, rows, rows, P(), P(), P(), P()), out_specs=rows, check_vma=False,
    )
```

time: 1290 us -> 177 us (0.14)
  matrix products: 419 us -> 0 us
  other arithmetic: 329 us -> 0.78 us
  waiting for transfers between devices: 306 us -> 9.41 us
  local copies, waits for them, and re-layouts: 120 us -> 5.31 us
  Pallas kernels: 0 us -> 84 us
  starting transfers between devices: 78.2 us -> 11 us
  blocking collectives: 24.7 us -> 66 us
    dot_general x289 -> x0, matrix products: 403 us -> none  [the longest x32 61.6 us: run_advance(): jnp.einsum('jel,jlm->jem', query_tiles, present_value, precision=peak_level)]
    another operation x6 -> x1, other arithmetic: 274 us -> 0.73 us  [shards(): jnp.stack([lax.ppermute(total, 'x', [(i, i + d) for i in range(nx - d)])...]
    ppermute x32 -> x4, waiting for transfers between devices: 249 us -> 9.41 us  [the longest x1 4.83 us: shards(): lax.ppermute(rim, ('x', 'z', 'c', 'y'), [(i, i + 1) for i in range(every...]
    pallas_call x0 -> x4, Pallas kernels: none -> 84 us  [the longest x1 67.7 us: shards(): pl.pallas_call(functools.partial(front_kernel, heads), grid=(head_count /...]
    all_to_all x4 -> x0, waiting for transfers between devices: 57.6 us -> none  [the longest x1 22.4 us: shards(): lax.all_to_all(k_in, 'head', split_axis=1, concat_axis=0, tiled=True)]
    ppermute x32 -> x4, starting transfers between devices: 61.6 us -> 11 us  [the longest x3 7.49 us: shards(): lax.ppermute(total, 'x', [(i, i + d) for i in range(nx - d)])]
    all_to_all x1 -> x2, blocking collectives: 24.7 us -> 66 us  [the longest x1 44.3 us: shards(): segment = lax.all_to_all(segment, around, 0, 0, tiled=True)]
    mul x5 -> x0, local copies, waits for them, and re-layouts: 20.5 us -> none  [the longest x2 10.5 us: unit_rows(): vectors * vectors]
  transfers between devices with their start and end apart: 36 -> 4, of which waited for: 35 -> 3; matrix products, arithmetic and copies ran while one was open for 2% -> 1% of each run, Pallas kernels for 0% -> 0%
where the time goes in v1:
time: 177 us
  Pallas kernels  84 us (47%)
  blocking collectives  66 us (37%)
  starting transfers between devices  11 us (6%)
  waiting for transfers between devices  9.41 us (5%)
  local copies, waits for them, and re-layouts  5.31 us (3%)
    pallas_call x1, Pallas kernels, shards(): pl.pallas_call(functools.partial(front_kernel, heads), grid=(head_count /...  67.7 us
    all_to_all x1, blocking collectives, shards(): segment = lax.all_to_all(segment, around, 0, 0, tiled=True)  44.3 us
    all_to_all x1, blocking collectives, shards(): lax.all_to_all(states, around, 0, 0, tiled=True)  21.7 us
    ppermute x3, starting transfers between devices, shards(): lax.ppermute(total, 'x', [(i, i + d) for i in range(nx - d)])  7.49 us
    pallas_call x1, Pallas kernels, shards(): pl.pallas_call(functools.partial(end_kernel, heads), grid=(head_count //...  7.13 us
    pallas_call x1, Pallas kernels, shards(): pl.pallas_call(functools.partial(gather_kernel, ny), out_shape=[jax.Shape...  5.09 us
    ppermute x1, waiting for transfers between devices, shards(): lax.ppermute(rim, ('x', 'z', 'c', 'y'), [(i, i + 1) for i in range(every...  4.83 us
    ppermute x3, waiting for transfers between devices, shards(): lax.ppermute(total, 'x', [(i, i + d) for i in range(nx - d)])  4.57 us
  transfers between devices with their start and end apart: 4, of which 3 were waited for; matrix products, arithmetic and copies ran while one was open for 1% of the time, Pallas kernels for 0%

profile of v1, /device:TPU:2, one launch (start us, length us, event | category | flops | bytes accessed | tf_op | source)
XLA Modules:
  0.0 176.5 jit_solution(15213507788941976390)
XLA Ops:
  0.0 0.8 slice.12
  0.8 0.8 slice.13
  1.5 0.8 slice.14
  2.4 3.5 %collective-permute-start = (bf16[9,2048]{1,0:T(8,128)(2,1)S(1)}, bf16[9,2048]{1,0:T(8,128)(2,1)S(1)}, u32[]{:S(2)}, u32[]{:S(2)}) collective-permute-start(bf16[9,2048]{1,0:T(8,128)(2,1)S(1)} %pad_maximum_fusion.1), channel_id=1, source_target_pairs={{0,1},{1,2},{2,3},{3,4},{4,5},{5,6},{6,7},{7,8},{8,9},{9,10},{10,1... | collective-permute-start | bytes 110600 | tf_op jit(solution)/shard_map/ppermute | solution.py:190
  5.9 1.5 copy.9.beta_ref
  7.3 4.8 %collective-permute-done.rim_ref = bf16[9,2048]{1,0:T(8,128)(2,1)S(1)} collective-permute-done((bf16[9,2048]{1,0:T(8,128)(2,1)S(1)}, bf16[9,2048]{1,0:T(8,128)(2,1)S(1)}, u32[]{:S(2)}, u32[]{:S(2)}) %collective-permute-start) | collective-permute-done | bytes 36896 | tf_op jit(solution)/shard_map/ppermute | solution.py:190
  12.2 0.0 copy-start
  12.2 0.6 copy-done
  12.8 67.7 %shard_map.82 = (f32[32,192,128]{2,1,0:T(8,128)}, f32[512,2048]{1,0:T(8,128)}, f32[512,2048]{1,0:T(8,128)}) custom-call(bf16[512,2048]{1,0:T(8,128)(2,1)} %q_ref.1, bf16[512,2048]{1,0:T(8,128)(2,1)} %k_ref.1, bf16[512,2048]{1,0:T(8,128)(2,1)} %v_ref.1, bf16[9,2048]{1,0:T(8,128)(2,1)} %copy-done, bf16[512,16]{1,0:T(8,128)(2,1)} %copy.9.beta_ref, ...), custom_call_target="tpu_custom_call" | custom-call | tf_op jit(solution)/shard_map/pallas_call | solution.py:198
  80.5 44.3 %all_to_all.10.seg_ref = f32[32,192,128]{2,1,0:T(8,128)} all-to-all(f32[32,192,128]{2,1,0:T(8,128)} %get-tuple-element.12), channel_id=1, replica_groups=mesh['x'=4,'z'=4,'c'=2,'y'=4] {'z','c','y'}, dimensions={0} | all-to-all | bytes 6291456 | tf_op jit(solution)/shard_map/all_to_all | solution.py:212
  124.9 5.1 %shard_map.83 = (f32[32,192,128]{2,1,0:T(8,128)}, f32[8,192,128]{2,1,0:T(8,128)}) custom-call(f32[32,192,128]{2,1,0:T(8,128)} %all_to_all.10.seg_ref), custom_call_target="tpu_custom_call" | custom-call | tf_op jit(solution)/shard_map/pallas_call | solution.py:213
  130.0 0.9 slice_bitcast_fusion
  130.9 0.7 collective-permute-start.3
  131.5 4.9 %collective-permute-start.2 = (f32[192,128]{1,0:T(8,128)S(1)}, f32[192,128]{1,0:T(8,128)S(1)}, u32[]{:S(2)}, u32[]{:S(2)}) collective-permute-start(f32[192,128]{1,0:T(8,128)S(1)} %slice_bitcast_fusion), channel_id=1, source_target_pairs={{0,64},{32,96},{1,65},{33,97},{2,66},{34,98},{3,67},{35,99},{4,68}... | collective-permute-start | bytes 294920 | tf_op jit(solution)/shard_map/ppermute | solution.py:221
  136.5 1.9 %collective-permute-start.1 = (f32[192,128]{1,0:T(8,128)S(1)}, f32[192,128]{1,0:T(8,128)S(1)}, u32[]{:S(2)}, u32[]{:S(2)}) collective-permute-start(f32[192,128]{1,0:T(8,128)S(1)} %slice_bitcast_fusion), channel_id=1, source_target_pairs={{0,32},{32,64},{64,96},{1,33},{33,65},{65,97},{2,34},{34,66},{66,9... | collective-permute-start | bytes 294920 | tf_op jit(solution)/shard_map/ppermute | solution.py:221
  138.4 0.0 collective-permute-done.3
  138.4 0.3 collective-permute-done.2
  138.6 4.3 %collective-permute-done.1 = f32[192,128]{1,0:T(8,128)S(1)} collective-permute-done((f32[192,128]{1,0:T(8,128)S(1)}, f32[192,128]{1,0:T(8,128)S(1)}, u32[]{:S(2)}, u32[]{:S(2)}) %collective-permute-start.1) | collective-permute-done | bytes 98336 | tf_op jit(solution)/shard_map/ppermute | solution.py:221
  143.0 0.7 pad_maximum_fusion.far_ref
  143.7 4.0 %shard_map.84 = f32[32,64,128]{2,1,0:T(8,128)} custom-call(f32[32,192,128]{2,1,0:T(8,128)} %get-tuple-element.13.loc_ref, f32[8,192,128]{2,1,0:T(8,128)} %get-tuple-element.14.grp_ref, f32[3,192,128]{2,1,0:T(8,128)} %pad_maximum_fusion.far_ref), custom_call_target="tpu_custom_call" | custom-call | tf_op jit(solution)/shard_map/pallas_call | solution.py:223
  147.7 21.7 %all_to_all.11 = f32[32,64,128]{2,1,0:T(8,128)} all-to-all(f32[32,64,128]{2,1,0:T(8,128)} %shard_map.84), channel_id=1, replica_groups=mesh['x'=4,'z'=4,'c'=2,'y'=4] {'z','c','y'}, dimensions={0} | all-to-all | bytes 2097152 | tf_op jit(solution)/shard_map/all_to_all | solution.py:228
  169.4 7.1 %shard_map.85 = bf16[512,2048]{1,0:T(8,128)(2,1)} custom-call(f32[512,2048]{1,0:T(8,128)} %get-tuple-element.10.qe_ref, f32[512,2048]{1,0:T(8,128)} %get-tuple-element.11.ol_ref, f32[16,128,128]{2,1,0:T(8,128)} %bitcast.7, f32[1,128]{1,0:T(1,128)} %bitcast.11), custom_call_target="tpu_custom_call" | custom-call | tf_op jit(solution)/shard_map/pallas_call | solution.py:232
  (1 shorter events, 0.0 us)
Async XLA Ops:
  2.4 9.8 %collective-permute-start = (bf16[9,2048]{1,0:T(8,128)(2,1)S(1)}, bf16[9,2048]{1,0:T(8,128)(2,1)S(1)}, u32[]{:S(2)}, u32[]{:S(2)}) collective-permute-start(bf16[9,2048]{1,0:T(8,128)(2,1)S(1)} %pad_maximum_fusion.1), channel_id=1, source_target_pairs={{0,1},{1,2},{2,3},{3,4},{4,5},{5,6},{6,7},{7,8},{8,9},{9,10},{10,1... | collective-permute-start | bytes 110600 | tf_op jit(solution)/shard_map/ppermute | solution.py:190
  12.2 0.6 copy-start
  130.9 7.5 %collective-permute-start.3 = (f32[192,128]{1,0:T(8,128)S(1)}, f32[192,128]{1,0:T(8,128)S(1)}, u32[]{:S(2)}, u32[]{:S(2)}) collective-permute-start(f32[192,128]{1,0:T(8,128)S(1)} %slice_bitcast_fusion), channel_id=1, source_target_pairs={{0,96},{1,97},{2,98},{3,99},{4,100},{5,101},{6,102},{7,103},{8,104... | collective-permute-start | bytes 294920 | tf_op jit(solution)/shard_map/ppermute | solution.py:221
  131.5 7.1 %collective-permute-start.2 = (f32[192,128]{1,0:T(8,128)S(1)}, f32[192,128]{1,0:T(8,128)S(1)}, u32[]{:S(2)}, u32[]{:S(2)}) collective-permute-start(f32[192,128]{1,0:T(8,128)S(1)} %slice_bitcast_fusion), channel_id=1, source_target_pairs={{0,64},{32,96},{1,65},{33,97},{2,66},{34,98},{3,67},{35,99},{4,68}... | collective-permute-start | bytes 294920 | tf_op jit(solution)/shard_map/ppermute | solution.py:221
  136.5 6.5 %collective-permute-start.1 = (f32[192,128]{1,0:T(8,128)S(1)}, f32[192,128]{1,0:T(8,128)S(1)}, u32[]{:S(2)}, u32[]{:S(2)}) collective-permute-start(f32[192,128]{1,0:T(8,128)S(1)} %slice_bitcast_fusion), channel_id=1, source_target_pairs={{0,32},{32,64},{64,96},{1,33},{33,65},{65,97},{2,34},{34,66},{66,9... | collective-permute-start | bytes 294920 | tf_op jit(solution)/shard_map/ppermute | solution.py:221

commit v2 on v1

--- a/solution.py
+++ b/solution.py
@@ -12,8 +12,6 @@
 KW = 4
 F32 = jnp.float32
 BF16 = jnp.bfloat16
-HEADS_PER_STEP = 4
-HEADS_PER_END = 4
 
 
 def dot(a, b, ca, cb):
@@ -35,12 +33,22 @@
     return dot(cat([ah, al], 1), cat([bh, bh], cb), 1, cb) + dot(ah, bl, 1, cb)
 
 
+def mm_thin(a, b):
+    return dot(a[0], b[0], 1, 0) + dot(a[0], b[1], 1, 0) + dot(a[1], b[0], 1, 0)
+
+
 def left(a):
     return cat([a[0], a[0], a[1]], 1)
 
 
 def right(b):
     return cat([b[0], b[1], b[0]], 0)
+
+
+def rim_kernel(q_ref, k_ref, v_ref, out_ref):
+    edge = KW - 1
+    for n, ref in enumerate((q_ref, k_ref, v_ref)):
+        out_ref[n * edge : (n + 1) * edge, :] = ref[...].astype(F32)[-edge:].astype(BF16)
 
 
 def front_kernel(heads, q_ref, k_ref, v_ref, rim_ref, beta_ref, cq_ref, ck_ref, cv_ref, tb_ref, qe_ref, ol_ref, pad_ref):
@@ -95,11 +103,11 @@
         inv[u] = one - jnp.where(masks[0], gram[u], 0.0)
     for n in range(1, 6):
         parts = {u: split(inv[u]) for u in units}
-        moved = {u: dot(left(split(jnp.where(masks[n], gram[u], 0.0))), right(parts[u]), 1, 0) for u in units}
-        inv = {u: inv[u] - dot(left(parts[u]), right(split(moved[u])), 1, 0) for u in units}
+        moved = {u: mm_thin(split(jnp.where(masks[n], gram[u], 0.0)), parts[u]) for u in units}
+        inv = {u: inv[u] - mm_thin(parts[u], split(moved[u])) for u in units}
     step, extra, eff, local = {}, {}, {}, {}
     for u in units:
-        solved = dot(left(split(inv[u])), right(split(kv_scaled[u])), 1, 0)
+        solved = mm_thin(split(inv[u]), split(kv_scaled[u]))
         signed = cat([-solved[:, :WIDTH], solved[:, WIDTH:]], 1)
         rhs = right(split(signed))
         kh, kl = ks[u]
@@ -127,8 +135,8 @@
         turned = state[i][:, :WIDTH].T
         added = state[i][:, WIDTH:].T
         for s in range(2):
-            tb_ref[2 * i + s, :WIDTH, :] = turned
-            tb_ref[2 * i + s, WIDTH:, :] = added[s * half : (s + 1) * half]
+            tb_ref[s * heads + i, :half, :] = turned[s * half : (s + 1) * half]
+            tb_ref[s * heads + i, half:, :] = added[s * half : (s + 1) * half]
 
 
 def joined(first, second):
@@ -136,8 +144,14 @@
     return out[:WIDTH], out[WIDTH:] + second[WIDTH:]
 
 
-def gather_kernel(group, seg_ref, loc_ref, grp_ref):
+def gather_kernel(group, core_ref, got_ref, other_ref, loc_ref, grp_ref, tot_ref, seg_ref):
+    half = WIDTH // 2
     groups = seg_ref.shape[0] // group
+    mine = pl.ds(pl.multiple_of(core_ref[0] * half, half), half)
+    theirs = pl.ds(pl.multiple_of((1 - core_ref[0]) * half, half), half)
+    seg_ref[:, mine, :] = got_ref[:, :half, :]
+    seg_ref[:, theirs, :] = other_ref[...]
+    seg_ref[:, WIDTH:, :] = got_ref[:, half:, :]
     for g in range(groups):
         loc_ref[g * group] = seg_ref[g * group]
     for j in range(1, group):
@@ -151,18 +165,19 @@
     for g in range(1, groups):
         run = cat(joined(run, loc_ref[g * group + group - 1]), 0)
         grp_ref[g] = run
-
-
-def spread_kernel(group, loc_ref, grp_ref, far_ref, out_ref):
+    tot_ref[...] = run
+
+
+def spread_kernel(group, loc_ref, grp_ref, *rest):
+    far, out_ref = rest[:-1], rest[-1]
     groups = loc_ref.shape[0] // group
-    reach = far_ref.shape[0]
 
     def through(state, place):
         return mm_wide(split(state), split(place[:WIDTH]), 0) + place[WIDTH:]
 
-    begin = far_ref[reach - 1, WIDTH:, :]
-    for d in range(reach - 2, -1, -1):
-        begin = through(begin, far_ref[d])
+    begin = far[-1][WIDTH:, :]
+    for place in far[-2::-1]:
+        begin = through(begin, place[...])
     heads_of = [begin] + [through(begin, grp_ref[g]) for g in range(groups - 1)]
     for g in range(groups):
         out_ref[g * group] = heads_of[g]
@@ -174,7 +189,7 @@
 def end_kernel(heads, qe_ref, ol_ref, st_ref, gain_ref, out_ref):
     for i in range(heads):
         lanes = slice(i * WIDTH, (i + 1) * WIDTH)
-        full = ol_ref[:, lanes] + mm_wide(split(qe_ref[:, lanes]), split(st_ref[i]), 1)
+        full = ol_ref[:, lanes] + mm_wide(split(qe_ref[:, lanes]), split(cat([st_ref[i], st_ref[heads + i]], 0)), 1)
         mean = jnp.mean(full * full, axis=-1, keepdims=True)
         out_ref[:, lanes] = (full * lax.rsqrt(mean + 1e-05) * gain_ref[...]).astype(BF16)
 
@@ -186,10 +201,17 @@
     head_count = beta.shape[1]
     pieces = 2 * head_count
     every = nx * nz * nc * ny
-    rim = cat([q_in[-edge:], k_in[-edge:], v_in[-edge:]], 0)
+    last = pl.BlockSpec((16, width), lambda i: (length // 16 - 1, 0))
+    rim = pl.pallas_call(
+        rim_kernel,
+        grid=(1,),
+        in_specs=[last] * 3,
+        out_specs=pl.BlockSpec((3 * edge, width), lambda i: (0, 0)),
+        out_shape=jax.ShapeDtypeStruct((3 * edge, width), BF16),
+    )(q_in, k_in, v_in)
     rim = lax.ppermute(rim, ("x", "z", "c", "y"), [(i, i + 1) for i in range(every - 1)])
 
-    heads = min(HEADS_PER_STEP, head_count)
+    heads = head_count // nz
     wide = heads * WIDTH
     body = pl.BlockSpec((length, wide), lambda i: (0, i))
     taps = pl.BlockSpec((KW, wide), lambda i: (0, i))
@@ -200,8 +222,8 @@
         grid=(head_count // heads,),
         in_specs=[body, body, body, pl.BlockSpec((3 * edge, wide), lambda i: (0, i)),
                   pl.BlockSpec((length, head_count), lambda i: (0, 0)), taps, taps, taps],
-        out_specs=[pl.BlockSpec((2 * heads, rows, WIDTH), lambda i: (i, 0, 0)), body, body],
-        out_shape=[jax.ShapeDtypeStruct((pieces, rows, WIDTH), F32),
+        out_specs=[pl.BlockSpec((2 * heads, WIDTH, WIDTH), lambda i: (i, 0, 0)), body, body],
+        out_shape=[jax.ShapeDtypeStruct((pieces, WIDTH, WIDTH), F32),
                    jax.ShapeDtypeStruct((length, width), F32),
                    jax.ShapeDtypeStruct((length, width), F32)],
         scratch_shapes=[pltpu.VMEM((3, 8 + length, wide), F32)],
@@ -210,29 +232,31 @@
 
     around = ("z", "c", "y")
     segment = lax.all_to_all(segment, around, 0, 0, tiled=True)
-    loc, grp = pl.pallas_call(
+    other = lax.ppermute(segment[:, : WIDTH // 2], "c", [(0, 1), (1, 0)])
+    loc, grp, total = pl.pallas_call(
         functools.partial(gather_kernel, ny),
+        in_specs=[pl.BlockSpec(memory_space=pltpu.SMEM), pl.BlockSpec(memory_space=pltpu.VMEM),
+                  pl.BlockSpec(memory_space=pltpu.VMEM)],
+        scratch_shapes=[pltpu.VMEM((pieces, rows, WIDTH), F32)],
         out_shape=[jax.ShapeDtypeStruct((pieces, rows, WIDTH), F32),
-                   jax.ShapeDtypeStruct((pieces // ny, rows, WIDTH), F32)],
-        compiler_params=vmem,
-    )(segment)
-    total = grp[-1]
-    far = jnp.stack([
-        lax.ppermute(total, "x", [(i, i + d) for i in range(nx - d)]) for d in range(1, nx)
-    ])
+                   jax.ShapeDtypeStruct((pieces // ny, rows, WIDTH), F32),
+                   jax.ShapeDtypeStruct((rows, WIDTH), F32)],
+        compiler_params=vmem,
+    )(lax.axis_index("c").astype(jnp.int32).reshape(1), segment, other)
+    far = [lax.ppermute(total, "x", [(i, i + d) for i in range(nx - d)]) for d in range(1, nx)]
     states = pl.pallas_call(
         functools.partial(spread_kernel, ny),
         out_shape=jax.ShapeDtypeStruct((pieces, WIDTH // 2, WIDTH), F32),
         compiler_params=vmem,
-    )(loc, grp, far)
-    states = lax.all_to_all(states, around, 0, 0, tiled=True).reshape(head_count, WIDTH, WIDTH)
-
-    heads = min(HEADS_PER_END, head_count)
+    )(loc, grp, *far)
+    states = lax.all_to_all(states, around, 0, 0, tiled=True)
+
+    heads = head_count // nz
     body = pl.BlockSpec((length, heads * WIDTH), lambda i: (0, i))
     return pl.pallas_call(
         functools.partial(end_kernel, heads),
         grid=(head_count // heads,),
-        in_specs=[body, body, pl.BlockSpec((heads, WIDTH, WIDTH), lambda i: (i, 0, 0)),
+        in_specs=[body, body, pl.BlockSpec((2 * heads, WIDTH // 2, WIDTH), lambda i: (i, 0, 0)),
                   pl.BlockSpec((1, WIDTH), lambda i: (0, 0))],
         out_specs=body,
         out_shape=jax.ShapeDtypeStruct((length, width), BF16),

time: 177 us -> 162 us (0.915)
  blocking collectives: 66 us -> 54.7 us
  Pallas kernels: 84 us -> 78.3 us
  waiting for transfers between devices: 9.41 us -> 13.4 us
    all_to_all x1, blocking collectives: 44.3 us -> 33 us  [shards(): segment = lax.all_to_all(segment, around, 0, 0, tiled=True)]
    pallas_call x1, Pallas kernels: 67.7 us -> 60.3 us  [shards(): pl.pallas_call(functools.partial(front_kernel, heads), grid=(head_count /...]
    ppermute x0 -> x1, waiting for transfers between devices: none -> 2.87 us  [shards(): other = lax.ppermute(segment[:, :WIDTH // 2], 'c', [(0, 1), (1, 0)])]
    pallas_call x1 -> x2, Pallas kernels: 5.09 us -> 6.86 us  [the longest x1 5.3 us: shards(): pl.pallas_call(functools.partial(gather_kernel, ny), in_specs=[pl.BlockSp...]
  transfers between devices with their start and end apart: 4 -> 5, of which waited for: 3 -> 4; matrix products, arithmetic and copies ran while one was open for 1% -> 0% of each run, Pallas kernels for 0% -> 0%
where the time goes in v2:
time: 162 us; the launch traced here: 161 us
  Pallas kernels  78.3 us (48%)
  blocking collectives  54.7 us (34%)
  waiting for transfers between devices  13.4 us (8%)
  starting transfers between devices  10.7 us (7%)
  local copies, waits for them, and re-layouts  4.23 us (3%)
    pallas_call x1, Pallas kernels, shards(): pl.pallas_call(functools.partial(front_kernel, heads), grid=(head_count /...  60.3 us
    all_to_all x1, blocking collectives, shards(): segment = lax.all_to_all(segment, around, 0, 0, tiled=True)  33 us
    all_to_all x1, blocking collectives, shards(): states = lax.all_to_all(states, around, 0, 0, tiled=True)  21.7 us
    ppermute x3, starting transfers between devices, shards(): lax.ppermute(total, 'x', [(i, i + d) for i in range(nx - d)])  7.24 us
    pallas_call x1, Pallas kernels, shards(): pl.pallas_call(functools.partial(end_kernel, heads), grid=(head_count //...  7.03 us
    ppermute x1, waiting for transfers between devices, shards(): lax.ppermute(rim, ('x', 'z', 'c', 'y'), [(i, i + 1) for i in range(every...  5.75 us
    pallas_call x1, Pallas kernels, shards(): pl.pallas_call(functools.partial(gather_kernel, ny), in_specs=[pl.BlockSp...  5.3 us
    ppermute x3, waiting for transfers between devices, shards(): lax.ppermute(total, 'x', [(i, i + d) for i in range(nx - d)])  4.77 us
  transfers between devices with their start and end apart: 5, of which 4 were waited for; matrix products, arithmetic and copies ran while one was open for 0% of the time, Pallas kernels for 0%

profile of v2, /device:TPU:2, one launch (start us, length us, event | category | flops | bytes accessed | tf_op | source)
XLA Modules:
  0.0 161.4 jit_solution(11042476388284239345)
XLA Ops:
  0.0 0.0 copy-start.6
  0.0 1.6 shard_map.82
  1.6 3.5 %collective-permute-start = (bf16[9,2048]{1,0:T(8,128)(2,1)}, bf16[9,2048]{1,0:T(8,128)(2,1)S(1)}, u32[]{:S(2)}, u32[]{:S(2)}) collective-permute-start(bf16[9,2048]{1,0:T(8,128)(2,1)} %shard_map.82), channel_id=1, source_target_pairs={{0,1},{1,2},{2,3},{3,4},{4,5},{5,6},{6,7},{7,8},{8,9},{9,10},{10,1... | collective-permute-start | bytes 110600 | tf_op jit(solution)/shard_map/ppermute | solution.py:212
  5.0 0.0 copy-done.6
  5.1 0.8 copy.9.beta_ref
  5.8 5.8 %collective-permute-done.rim_ref = bf16[9,2048]{1,0:T(8,128)(2,1)S(1)} collective-permute-done((bf16[9,2048]{1,0:T(8,128)(2,1)}, bf16[9,2048]{1,0:T(8,128)(2,1)S(1)}, u32[]{:S(2)}, u32[]{:S(2)}) %collective-permute-start) | collective-permute-done | bytes 36896 | tf_op jit(solution)/shard_map/ppermute | solution.py:212
  11.6 0.0 copy-start.5
  11.6 0.6 copy-done.5
  12.2 60.3 %shard_map.83 = (f32[32,128,128]{2,1,0:T(8,128)}, f32[512,2048]{1,0:T(8,128)}, f32[512,2048]{1,0:T(8,128)}) custom-call(bf16[512,2048]{1,0:T(8,128)(2,1)} %q_ref.3, bf16[512,2048]{1,0:T(8,128)(2,1)} %k_ref.3, bf16[512,2048]{1,0:T(8,128)(2,1)} %v_ref.3, bf16[9,2048]{1,0:T(8,128)(2,1)} %copy-done.5, bf16[512,16]{1,0:T(8,128)(2,1)} %copy.9.beta_ref, ...), custom_call_target="tpu_custom_call" | custom-call | tf_op jit(solution)/shard_map/pallas_call | solution.py:220
  72.5 33.0 %all_to_all.10.got_ref = f32[32,128,128]{2,1,0:T(8,128)S(1)} all-to-all(f32[32,128,128]{2,1,0:T(8,128)} %get-tuple-element.13), channel_id=1, replica_groups=mesh['x'=4,'z'=4,'c'=2,'y'=4] {'z','c','y'}, dimensions={0} | all-to-all | bytes 4194304 | tf_op jit(solution)/shard_map/all_to_all | solution.py:234
  105.5 0.0 copy-start
  105.5 1.2 slice.4
  106.7 0.0 collective-permute-start.1
  106.7 2.9 %collective-permute-done.1.other_ref = f32[32,64,128]{2,1,0:T(8,128)S(1)} collective-permute-done((f32[32,64,128]{2,1,0:T(8,128)}, f32[32,64,128]{2,1,0:T(8,128)S(1)}, u32[]{:S(2)}, u32[]{:S(2)}) %collective-permute-start.1) | collective-permute-done | bytes 1048608 | tf_op jit(solution)/shard_map/ppermute | solution.py:235
  109.6 0.0 copy-start.1
  109.6 0.0 copy-done
  109.6 1.0 copy-done.1
  110.6 5.3 %shard_map.84 = (f32[32,192,128]{2,1,0:T(8,128)}, f32[8,192,128]{2,1,0:T(8,128)}, f32[192,128]{1,0:T(8,128)}) custom-call(s32[1]{0:T(128)} %bitcast.core_ref, f32[32,128,128]{2,1,0:T(8,128)} %copy-done, f32[32,64,128]{2,1,0:T(8,128)} %copy-done.1), custom_call_target="tpu_custom_call" | custom-call | tf_op jit(solution)/shard_map/pallas_call | solution.py:236
  115.9 0.7 collective-permute-start.4
  116.6 4.7 %collective-permute-start.3 = (f32[192,128]{1,0:T(8,128)}, f32[192,128]{1,0:T(8,128)S(1)}, u32[]{:S(2)}, u32[]{:S(2)}) collective-permute-start(f32[192,128]{1,0:T(8,128)} %get-tuple-element.16), channel_id=1, source_target_pairs={{0,64},{32,96},{1,65},{33,97},{2,66},{34,98},{3,67},{35,99},{4,68}... | collective-permute-start | bytes 294920 | tf_op jit(solution)/shard_map/ppermute | solution.py:246
  121.2 1.9 %collective-permute-start.2 = (f32[192,128]{1,0:T(8,128)}, f32[192,128]{1,0:T(8,128)S(1)}, u32[]{:S(2)}, u32[]{:S(2)}) collective-permute-start(f32[192,128]{1,0:T(8,128)} %get-tuple-element.16), channel_id=1, source_target_pairs={{0,32},{32,64},{64,96},{1,33},{33,65},{65,97},{2,34},{34,66},{66,9... | collective-permute-start | bytes 294920 | tf_op jit(solution)/shard_map/ppermute | solution.py:246
  123.2 0.0 collective-permute-done.4.rest_2_
  123.2 0.0 copy-start.2
  123.2 0.7 collective-permute-done.3.rest_1_
  123.9 0.0 copy-start.3
  123.9 4.0 %collective-permute-done.2.rest_0_ = f32[192,128]{1,0:T(8,128)S(1)} collective-permute-done((f32[192,128]{1,0:T(8,128)}, f32[192,128]{1,0:T(8,128)S(1)}, u32[]{:S(2)}, u32[]{:S(2)}) %collective-permute-start.2) | collective-permute-done | bytes 98336 | tf_op jit(solution)/shard_map/ppermute | solution.py:246
  128.0 0.0 copy-done.2
  128.0 0.0 copy-done.3
  128.0 0.6 copy-done.4
  128.6 4.1 %shard_map.85 = f32[32,64,128]{2,1,0:T(8,128)} custom-call(f32[32,192,128]{2,1,0:T(8,128)} %get-tuple-element.14.loc_ref, f32[8,192,128]{2,1,0:T(8,128)} %get-tuple-element.15.grp_ref, f32[192,128]{1,0:T(8,128)} %copy-done.4, f32[192,128]{1,0:T(8,128)} %copy-done.3, f32[192,128]{1,0:T(8,128)} %copy-done.2), custom_call_target="tpu_custom_call" | custom-call | tf_op jit(solution)/shard_map/pallas_call | solution.py:247
  132.7 21.7 %all_to_all.11.st_ref = f32[32,64,128]{2,1,0:T(8,128)} all-to-all(f32[32,64,128]{2,1,0:T(8,128)} %shard_map.85), channel_id=1, replica_groups=mesh['x'=4,'z'=4,'c'=2,'y'=4] {'z','c','y'}, dimensions={0} | all-to-all | bytes 2097152 | tf_op jit(solution)/shard_map/all_to_all | solution.py:252
  154.3 7.0 %shard_map.86 = bf16[512,2048]{1,0:T(8,128)(2,1)} custom-call(f32[512,2048]{1,0:T(8,128)} %get-tuple-element.11.qe_ref, f32[512,2048]{1,0:T(8,128)} %get-tuple-element.12.ol_ref, f32[32,64,128]{2,1,0:T(8,128)} %all_to_all.11.st_ref, f32[1,128]{1,0:T(1,128)} %bitcast.2), custom_call_target="tpu_custom_call" | custom-call | tf_op jit(solution)/shard_map/pallas_call | solution.py:256
  (1 shorter events, 0.0 us)
Async XLA Ops:
  0.0 5.1 %copy-start.6 = (bf16[512,16]{0,1:T(8,128)(2,1)S(1)}, bf16[512,16]{0,1:T(8,128)(2,1)}, u32[]{:S(2)}) copy-start(bf16[512,16]{0,1:T(8,128)(2,1)} %param.11) | copy-start | bytes 49156
  1.6 10.0 %collective-permute-start = (bf16[9,2048]{1,0:T(8,128)(2,1)}, bf16[9,2048]{1,0:T(8,128)(2,1)S(1)}, u32[]{:S(2)}, u32[]{:S(2)}) collective-permute-start(bf16[9,2048]{1,0:T(8,128)(2,1)} %shard_map.82), channel_id=1, source_target_pairs={{0,1},{1,2},{2,3},{3,4},{4,5},{5,6},{6,7},{7,8},{8,9},{9,10},{10,1... | collective-permute-start | bytes 110600 | tf_op jit(solution)/shard_map/ppermute | solution.py:212
  11.6 0.6 copy-start.5
  105.5 4.1 %copy-start = (f32[32,128,128]{2,1,0:T(8,128)}, f32[32,128,128]{2,1,0:T(8,128)S(1)}, u32[]{:S(2)}) copy-start(f32[32,128,128]{2,1,0:T(8,128)S(1)} %all_to_all.10.got_ref) | copy-start | bytes 6291460
  106.7 2.9 %collective-permute-start.1 = (f32[32,64,128]{2,1,0:T(8,128)}, f32[32,64,128]{2,1,0:T(8,128)S(1)}, u32[]{:S(2)}, u32[]{:S(2)}) collective-permute-start(f32[32,64,128]{2,1,0:T(8,128)} %slice.4), channel_id=1, source_target_pairs={{0,4},{4,0},{1,5},{5,1},{2,6},{6,2},{3,7},{7,3},{8,12},{12,8},{9,1... | collective-permute-start | bytes 3145736 | tf_op jit(solution)/shard_map/ppermute | solution.py:235
  109.6 1.0 copy-start.1
  115.9 7.3 %collective-permute-start.4 = (f32[192,128]{1,0:T(8,128)}, f32[192,128]{1,0:T(8,128)S(1)}, u32[]{:S(2)}, u32[]{:S(2)}) collective-permute-start(f32[192,128]{1,0:T(8,128)} %get-tuple-element.16), channel_id=1, source_target_pairs={{0,96},{1,97},{2,98},{3,99},{4,100},{5,101},{6,102},{7,103},{8,104... | collective-permute-start | bytes 294920 | tf_op jit(solution)/shard_map/ppermute | solution.py:246
  116.6 7.4 %collective-permute-start.3 = (f32[192,128]{1,0:T(8,128)}, f32[192,128]{1,0:T(8,128)S(1)}, u32[]{:S(2)}, u32[]{:S(2)}) collective-permute-start(f32[192,128]{1,0:T(8,128)} %get-tuple-element.16), channel_id=1, source_target_pairs={{0,64},{32,96},{1,65},{33,97},{2,66},{34,98},{3,67},{35,99},{4,68}... | collective-permute-start | bytes 294920 | tf_op jit(solution)/shard_map/ppermute | solution.py:246
  121.2 6.7 %collective-permute-start.2 = (f32[192,128]{1,0:T(8,128)}, f32[192,128]{1,0:T(8,128)S(1)}, u32[]{:S(2)}, u32[]{:S(2)}) collective-permute-start(f32[192,128]{1,0:T(8,128)} %get-tuple-element.16), channel_id=1, source_target_pairs={{0,32},{32,64},{64,96},{1,33},{33,65},{65,97},{2,34},{34,66},{66,9... | collective-permute-start | bytes 294920 | tf_op jit(solution)/shard_map/ppermute | solution.py:246
  123.2 4.8 %copy-start.2 = (f32[192,128]{1,0:T(8,128)}, f32[192,128]{1,0:T(8,128)S(1)}, u32[]{:S(2)}) copy-start(f32[192,128]{1,0:T(8,128)S(1)} %collective-permute-done.4.rest_2_) | copy-start | bytes 294916
  123.9 4.0 %copy-start.3 = (f32[192,128]{1,0:T(8,128)}, f32[192,128]{1,0:T(8,128)S(1)}, u32[]{:S(2)}) copy-start(f32[192,128]{1,0:T(8,128)S(1)} %collective-permute-done.3.rest_1_) | copy-start | bytes 294916
  128.0 0.6 copy-start.4

commit v3 on v2

--- a/solution.py
+++ b/solution.py
@@ -217,6 +217,7 @@
     taps = pl.BlockSpec((KW, wide), lambda i: (0, i))
     rows = WIDTH + WIDTH // 2
     vmem = pltpu.CompilerParams(vmem_limit_bytes=56 << 20)
+    small = pltpu.CompilerParams(vmem_limit_bytes=20 << 20)
     segment, qe, ol = pl.pallas_call(
         functools.partial(front_kernel, heads),
         grid=(head_count // heads,),
@@ -241,13 +242,13 @@
         out_shape=[jax.ShapeDtypeStruct((pieces, rows, WIDTH), F32),
                    jax.ShapeDtypeStruct((pieces // ny, rows, WIDTH), F32),
                    jax.ShapeDtypeStruct((rows, WIDTH), F32)],
-        compiler_params=vmem,
+        compiler_params=small,
     )(lax.axis_index("c").astype(jnp.int32).reshape(1), segment, other)
     far = [lax.ppermute(total, "x", [(i, i + d) for i in range(nx - d)]) for d in range(1, nx)]
     states = pl.pallas_call(
         functools.partial(spread_kernel, ny),
         out_shape=jax.ShapeDtypeStruct((pieces, WIDTH // 2, WIDTH), F32),
-        compiler_params=vmem,
+        compiler_params=small,
     )(loc, grp, *far)
     states = lax.all_to_all(states, around, 0, 0, tiled=True)
 
@@ -260,7 +261,7 @@
                   pl.BlockSpec((1, WIDTH), lambda i: (0, 0))],
         out_specs=body,
         out_shape=jax.ShapeDtypeStruct((length, width), BF16),
-        compiler_params=vmem,
+        compiler_params=small,
     )(qe, ol, states, out_gain.reshape(1, WIDTH))
 
 

time: 162 us -> 150 us (0.926)
  Pallas kernels: 78.3 us -> 69.5 us
  local copies, waits for them, and re-layouts: 4.23 us -> 2.43 us
    pallas_call x1, Pallas kernels: 4.06 us -> 0.91 us  [shards(): pl.pallas_call(functools.partial(spread_kernel, ny), out_shape=jax.ShapeD...]
    pallas_call x1, Pallas kernels: 5.3 us -> 2.43 us  [shards(): pl.pallas_call(functools.partial(gather_kernel, ny), in_specs=[pl.BlockSp...]
    pallas_call x1, Pallas kernels: 7.03 us -> 4.28 us  [shards(): pl.pallas_call(functools.partial(end_kernel, heads), grid=(head_count //...]
    unnamed x15 -> x11, local copies, waits for them, and re-layouts: 3.03 us -> 1.39 us
  transfers between devices with their start and end apart: 5 -> 5, of which waited for: 4 -> 4; matrix products, arithmetic and copies ran while one was open for 0% -> 1% of each run, Pallas kernels for 0% -> 0%
where the time goes in v3:
time: 150 us
  Pallas kernels  69.5 us (46%)
  blocking collectives  54.2 us (36%)
  waiting for transfers between devices  13.2 us (9%)
  starting transfers between devices  10.7 us (7%)
  local copies, waits for them, and re-layouts  2.43 us (2%)
    pallas_call x1, Pallas kernels, shards(): pl.pallas_call(functools.partial(front_kernel, heads), grid=(head_count /...  60.3 us
    all_to_all x1, blocking collectives, shards(): segment = lax.all_to_all(segment, around, 0, 0, tiled=True)  33 us
    all_to_all x1, blocking collectives, shards(): states = lax.all_to_all(states, around, 0, 0, tiled=True)  21.2 us
    ppermute x3, starting transfers between devices, shards(): lax.ppermute(total, 'x', [(i, i + d) for i in range(nx - d)])  7.25 us
    ppermute x1, waiting for transfers between devices, shards(): lax.ppermute(rim, ('x', 'z', 'c', 'y'), [(i, i + 1) for i in range(every...  5.75 us
    ppermute x3, waiting for transfers between devices, shards(): lax.ppermute(total, 'x', [(i, i + d) for i in range(nx - d)])  4.57 us
    pallas_call x1, Pallas kernels, shards(): pl.pallas_call(functools.partial(end_kernel, heads), grid=(head_count //...  4.28 us
    ppermute x1, starting transfers between devices, shards(): lax.ppermute(rim, ('x', 'z', 'c', 'y'), [(i, i + 1) for i in range(every...  3.47 us
  transfers between devices with their start and end apart: 5, of which 4 were waited for; matrix products, arithmetic and copies ran while one was open for 1% of the time, Pallas kernels for 0%

profile of v3, /device:TPU:2, one launch (start us, length us, event | category | flops | bytes accessed | tf_op | source)
XLA Modules:
  0.0 150.2 jit_solution(7186331845193327057)
XLA Ops:
  0.0 0.0 copy-start.4
  0.0 1.6 %shard_map.82 = bf16[9,2048]{1,0:T(8,128)(2,1)} custom-call(bf16[512,2048]{1,0:T(8,128)(2,1)} %q_ref.3, bf16[512,2048]{1,0:T(8,128)(2,1)} %k_ref.3, bf16[512,2048]{1,0:T(8,128)(2,1)} %v_ref.3), custom_call_target="tpu_custom_call" | custom-call | tf_op jit(solution)/shard_map/pallas_call | solution.py:205
  1.6 3.5 %collective-permute-start = (bf16[9,2048]{1,0:T(8,128)(2,1)}, bf16[9,2048]{1,0:T(8,128)(2,1)S(1)}, u32[]{:S(2)}, u32[]{:S(2)}) collective-permute-start(bf16[9,2048]{1,0:T(8,128)(2,1)} %shard_map.82), channel_id=1, source_target_pairs={{0,1},{1,2},{2,3},{3,4},{4,5},{5,6},{6,7},{7,8},{8,9},{9,10},{10,1... | collective-permute-start | bytes 110600 | tf_op jit(solution)/shard_map/ppermute | solution.py:212
  5.0 0.0 copy-done.4
  5.1 0.8 copy.9.beta_ref
  5.8 5.8 %collective-permute-done.rim_ref = bf16[9,2048]{1,0:T(8,128)(2,1)S(1)} collective-permute-done((bf16[9,2048]{1,0:T(8,128)(2,1)}, bf16[9,2048]{1,0:T(8,128)(2,1)S(1)}, u32[]{:S(2)}, u32[]{:S(2)}) %collective-permute-start) | collective-permute-done | bytes 36896 | tf_op jit(solution)/shard_map/ppermute | solution.py:212
  11.6 0.0 copy-start.3
  11.6 0.6 copy-done.3
  12.2 60.3 %shard_map.83 = (f32[32,128,128]{2,1,0:T(8,128)}, f32[512,2048]{1,0:T(8,128)}, f32[512,2048]{1,0:T(8,128)}) custom-call(bf16[512,2048]{1,0:T(8,128)(2,1)} %q_ref.3, bf16[512,2048]{1,0:T(8,128)(2,1)} %k_ref.3, bf16[512,2048]{1,0:T(8,128)(2,1)} %v_ref.3, bf16[9,2048]{1,0:T(8,128)(2,1)} %copy-done.3, bf16[512,16]{1,0:T(8,128)(2,1)} %copy.9.beta_ref, ...), custom_call_target="tpu_custom_call" | custom-call | tf_op jit(solution)/shard_map/pallas_call | solution.py:221
  72.5 33.0 %all_to_all.10.got_ref = f32[32,128,128]{2,1,0:T(8,128)S(1)} all-to-all(f32[32,128,128]{2,1,0:T(8,128)} %get-tuple-element.13), channel_id=1, replica_groups=mesh['x'=4,'z'=4,'c'=2,'y'=4] {'z','c','y'}, dimensions={0} | all-to-all | bytes 4194304 | tf_op jit(solution)/shard_map/all_to_all | solution.py:235
  105.5 1.0 slice.4
  106.6 0.0 collective-permute-start.1
  106.6 2.9 %collective-permute-done.1.other_ref = f32[32,64,128]{2,1,0:T(8,128)S(1)} collective-permute-done((f32[32,64,128]{2,1,0:T(8,128)}, f32[32,64,128]{2,1,0:T(8,128)S(1)}, u32[]{:S(2)}, u32[]{:S(2)}) %collective-permute-start.1) | collective-permute-done | bytes 1048608 | tf_op jit(solution)/shard_map/ppermute | solution.py:236
  109.4 0.0 copy-start.1
  109.4 2.4 %shard_map.84 = (f32[32,192,128]{2,1,0:T(8,128)S(1)}, f32[8,192,128]{2,1,0:T(8,128)S(1)}, f32[192,128]{1,0:T(8,128)S(1)}) custom-call(s32[1]{0:T(128)} %bitcast.core_ref, f32[32,128,128]{2,1,0:T(8,128)S(1)} %all_to_all.10.got_ref, f32[32,64,128]{2,1,0:T(8,128)S(1)} %collective-permute-done.1.other_ref), custom_call_target="tpu_custom_call" | custom-call | tf_op jit(solution)/shard_map/pallas_call | solution.py:237
  111.9 0.7 collective-permute-start.4
  112.5 4.7 %collective-permute-start.3 = (f32[192,128]{1,0:T(8,128)S(1)}, f32[192,128]{1,0:T(8,128)S(1)}, u32[]{:S(2)}, u32[]{:S(2)}) collective-permute-start(f32[192,128]{1,0:T(8,128)S(1)} %get-tuple-element.16), channel_id=1, source_target_pairs={{0,64},{32,96},{1,65},{33,97},{2,66},{34,98},{3,67},{35,99},{4,68}... | collective-permute-start | bytes 294920 | tf_op jit(solution)/shard_map/ppermute | solution.py:247
  117.2 1.9 %collective-permute-start.2 = (f32[192,128]{1,0:T(8,128)S(1)}, f32[192,128]{1,0:T(8,128)S(1)}, u32[]{:S(2)}, u32[]{:S(2)}) collective-permute-start(f32[192,128]{1,0:T(8,128)S(1)} %get-tuple-element.16), channel_id=1, source_target_pairs={{0,32},{32,64},{64,96},{1,33},{33,65},{65,97},{2,34},{34,66},{66,9... | collective-permute-start | bytes 294920 | tf_op jit(solution)/shard_map/ppermute | solution.py:247
  119.1 0.0 collective-permute-done.4.rest_2_
  119.2 0.4 collective-permute-done.3.rest_1_
  119.6 4.1 %collective-permute-done.2.rest_0_ = f32[192,128]{1,0:T(8,128)S(1)} collective-permute-done((f32[192,128]{1,0:T(8,128)S(1)}, f32[192,128]{1,0:T(8,128)S(1)}, u32[]{:S(2)}, u32[]{:S(2)}) %collective-permute-start.2) | collective-permute-done | bytes 98336 | tf_op jit(solution)/shard_map/ppermute | solution.py:247
  123.7 0.0 copy-start
  123.7 0.9 shard_map.85
  124.6 0.0 copy-start.2
  124.7 21.2 %all_to_all.11.st_ref = f32[32,64,128]{2,1,0:T(8,128)S(1)} all-to-all(f32[32,64,128]{2,1,0:T(8,128)S(1)} %shard_map.85), channel_id=1, replica_groups=mesh['x'=4,'z'=4,'c'=2,'y'=4] {'z','c','y'}, dimensions={0} | all-to-all | bytes 2097152 | tf_op jit(solution)/shard_map/all_to_all | solution.py:253
  145.9 0.0 copy-done.1
  145.9 0.0 copy-done
  145.9 0.0 copy-done.2
  145.9 4.3 %shard_map.86 = bf16[512,2048]{1,0:T(8,128)(2,1)} custom-call(f32[512,2048]{1,0:T(8,128)S(1)} %copy-done, f32[512,2048]{1,0:T(8,128)S(1)} %copy-done.1, f32[32,64,128]{2,1,0:T(8,128)S(1)} %all_to_all.11.st_ref, f32[1,128]{1,0:T(1,128)S(1)} %bitcast.2), custom_call_target="tpu_custom_call" | custom-call | tf_op jit(solution)/shard_map/pallas_call | solution.py:257
Async XLA Ops:
  0.0 5.1 %copy-start.4 = (bf16[512,16]{0,1:T(8,128)(2,1)S(1)}, bf16[512,16]{0,1:T(8,128)(2,1)}, u32[]{:S(2)}) copy-start(bf16[512,16]{0,1:T(8,128)(2,1)} %param.11) | copy-start | bytes 49156
  1.6 10.0 %collective-permute-start = (bf16[9,2048]{1,0:T(8,128)(2,1)}, bf16[9,2048]{1,0:T(8,128)(2,1)S(1)}, u32[]{:S(2)}, u32[]{:S(2)}) collective-permute-start(bf16[9,2048]{1,0:T(8,128)(2,1)} %shard_map.82), channel_id=1, source_target_pairs={{0,1},{1,2},{2,3},{3,4},{4,5},{5,6},{6,7},{7,8},{8,9},{9,10},{10,1... | collective-permute-start | bytes 110600 | tf_op jit(solution)/shard_map/ppermute | solution.py:212
  11.6 0.6 copy-start.3
  106.6 2.9 %collective-permute-start.1 = (f32[32,64,128]{2,1,0:T(8,128)}, f32[32,64,128]{2,1,0:T(8,128)S(1)}, u32[]{:S(2)}, u32[]{:S(2)}) collective-permute-start(f32[32,64,128]{2,1,0:T(8,128)} %slice.4), channel_id=1, source_target_pairs={{0,4},{4,0},{1,5},{5,1},{2,6},{6,2},{3,7},{7,3},{8,12},{12,8},{9,1... | collective-permute-start | bytes 3145736 | tf_op jit(solution)/shard_map/ppermute | solution.py:236
  109.4 36.4 %copy-start.1 = (f32[512,2048]{1,0:T(8,128)S(1)}, f32[512,2048]{1,0:T(8,128)}, u32[]{:S(2)}) copy-start(f32[512,2048]{1,0:T(8,128)} %get-tuple-element.12.ol_ref) | copy-start | bytes 12582916
  111.9 7.3 %collective-permute-start.4 = (f32[192,128]{1,0:T(8,128)S(1)}, f32[192,128]{1,0:T(8,128)S(1)}, u32[]{:S(2)}, u32[]{:S(2)}) collective-permute-start(f32[192,128]{1,0:T(8,128)S(1)} %get-tuple-element.16), channel_id=1, source_target_pairs={{0,96},{1,97},{2,98},{3,99},{4,100},{5,101},{6,102},{7,103},{8,104... | collective-permute-start | bytes 294920 | tf_op jit(solution)/shard_map/ppermute | solution.py:247
  112.5 7.0 %collective-permute-start.3 = (f32[192,128]{1,0:T(8,128)S(1)}, f32[192,128]{1,0:T(8,128)S(1)}, u32[]{:S(2)}, u32[]{:S(2)}) collective-permute-start(f32[192,128]{1,0:T(8,128)S(1)} %get-tuple-element.16), channel_id=1, source_target_pairs={{0,64},{32,96},{1,65},{33,97},{2,66},{34,98},{3,67},{35,99},{4,68}... | collective-permute-start | bytes 294920 | tf_op jit(solution)/shard_map/ppermute | solution.py:247
  117.2 6.5 %collective-permute-start.2 = (f32[192,128]{1,0:T(8,128)S(1)}, f32[192,128]{1,0:T(8,128)S(1)}, u32[]{:S(2)}, u32[]{:S(2)}) collective-permute-start(f32[192,128]{1,0:T(8,128)S(1)} %get-tuple-element.16), channel_id=1, source_target_pairs={{0,32},{32,64},{64,96},{1,33},{33,65},{65,97},{2,34},{34,66},{66,9... | collective-permute-start | bytes 294920 | tf_op jit(solution)/shard_map/ppermute | solution.py:247
  123.7 22.1 %copy-start = (f32[512,2048]{1,0:T(8,128)S(1)}, f32[512,2048]{1,0:T(8,128)}, u32[]{:S(2)}) copy-start(f32[512,2048]{1,0:T(8,128)} %get-tuple-element.11.qe_ref) | copy-start | bytes 12582916
  124.6 21.2 %copy-start.2 = (f32[128]{0:T(128)S(1)}, f32[128]{0:T(128)}, u32[]{:S(2)}) copy-start(f32[128]{0:T(128)} %param.15) | copy-start | bytes 1540
